TPU v7x, 512 devices: a whole 4x8x8 slice. The times are simulated.
512 devices in a mesh: ctx: 16 (over y, core), head: 8 (over z), rep: 4 (over x).
Axes of the slice: x: 4, y: 8, z: 8, core: 2. Of those that a mesh axis runs over, the one named last changes fastest.
Arguments:
- q_turn: bfloat16 [1024, 8192], P(('rep', 'ctx', 'head')), parts along dimension 0, may hold values from -18 to 18
- k_turn: bfloat16 [1024, 1024], P(('rep', 'ctx', 'head')), parts along dimension 0, may hold values from -6 to 6
- v_turn: bfloat16 [1024, 1024], P(('rep', 'ctx', 'head')), parts along dimension 0, may hold values from -6 to 6
- cache_k: bfloat16 [2048, 64, 1024], P(('rep', 'ctx'), None, 'head'), parts along dimension 0, may hold values from -6 to 6
- cache_v: bfloat16 [2048, 64, 1024], P(('rep', 'ctx'), None, 'head'), parts along dimension 0, may hold values from -6 to 6
- k_scale: float32 [2048, 8], P(('rep', 'ctx'), 'head'), parts along dimension 0, may hold values from 0.25 to 2
- v_scale: float32 [2048, 8], P(('rep', 'ctx'), 'head'), parts along dimension 0, may hold values from 0.25 to 2
- page_map: int32 [2048], P(('rep', 'ctx')), parts along dimension 0, may hold values from 0 to 511, as said below
Outputs:
- attn_out: bfloat16 [1024, 8192], P(('rep', 'ctx'), 'head'), parts along dimension 0
- cache_k_paired: bfloat16 [131072, 1024], P(('rep', 'ctx'), 'head'), parts along dimension 0
- cache_v_paired: bfloat16 [131072, 1024], P(('rep', 'ctx'), 'head'), parts along dimension 0
There are 4 independent parts, one for each index of `rep`. A program takes and returns all parts, laid end to end along the dimension named above; each array names one. Nothing has to cross between parts.
Inputs may be any that keep to these rules, and one draw needn't show every extreme that they name: A permutation: slot s holds logical page page_map[s]. Cut the 512 logical pages into 32 blocks of 16 consecutive pages; the 32 slots of each index of ctx hold exactly one page of every block.
All inputs are finite; a program needn't handle non-finite values.
Results may differ from a plain program's by a relative error of at most 0.0087.
Values may be sent and summed in bfloat16 or wider, within the bound.
No kernel may reach another device: no remote copies, remote signals or barrier semaphores. Data moves between devices by JAX's collectives and lax.ppermute only.
A program may use at most 64 MiB of HBM per device.

v0:
```python
import math

import jax
import jax.numpy as jnp
from jax import lax
from jax.experimental import pallas as pl
from jax.experimental.pallas import tpu as pltpu
from jax.sharding import PartitionSpec as P


INFO_ROWS = 8
BF16 = jnp.bfloat16
F32 = jnp.float32


def prepare_kernel(map_ref, k_scale_ref, v_scale_ref, k_ref, v_ref, send_ref, *, half, peers):
    slots, page_rows, width = k_ref.shape
    body_rows = 4 * page_rows
    row = lax.broadcasted_iota(jnp.int32, (INFO_ROWS, width), 0)

    def one_slot(slot, carry):
        page = map_ref[slot]
        block = page // half
        place = page - block * half
        upper = block >= peers
        owner = jnp.where(upper, 2 * peers - 1 - block, block)
        side = jnp.where(upper, 1, 0)
        at_k = pl.multiple_of(side * page_rows, page_rows)
        at_v = pl.multiple_of((2 + side) * page_rows, page_rows)
        send_ref[owner, pl.ds(at_k, page_rows), :] = (
            k_ref[slot].astype(F32) * k_scale_ref[slot]
        ).astype(BF16)
        send_ref[owner, pl.ds(at_v, page_rows), :] = (
            v_ref[slot].astype(F32) * v_scale_ref[slot]
        ).astype(BF16)
        info = send_ref[owner, body_rows : body_rows + INFO_ROWS, :].astype(F32)
        info = jnp.where(row == side, place.astype(F32), info)
        send_ref[owner, body_rows : body_rows + INFO_ROWS, :] = info.astype(BF16)
        return carry

    send_ref[:, body_rows:, :] = jnp.zeros((peers, INFO_ROWS, width), BF16)
    lax.fori_loop(0, slots, one_slot, 0)


def place_kernel(info_ref, recv_ref, k_ref, v_ref, *, half, page_rows):
    peers = recv_ref.shape[0]

    def one_peer(peer, carry):
        for side in range(2):
            at = info_ref[2 * peer + side] * page_rows + side * half * page_rows
            at = pl.multiple_of(at, page_rows)
            k_ref[pl.ds(at, page_rows), :] = recv_ref[peer, pl.ds(side * page_rows, page_rows), :]
            v_ref[pl.ds(at, page_rows), :] = recv_ref[
                peer, pl.ds((2 + side) * page_rows, page_rows), :
            ]
        return carry

    lax.fori_loop(0, peers, one_peer, 0)


def attend_kernel(
    start_ref, q_ref, kv_ref, tk_ref, tv_ref, msg_ref, s_even, s_odd, stat_ref, *, factor, keys_at_once
):
    peers, _, dim = kv_ref.shape
    length, width = q_ref.shape
    heads = width // dim
    own = tk_ref.shape[0]
    kv_rows = (kv_ref.shape[1] - INFO_ROWS) // 2
    per_chunk = keys_at_once // kv_rows
    chunks = peers // per_chunk
    log_factor = factor * math.log2(math.e)
    contract = (((1,), (1,)), ((), ()))
    lane = lax.broadcasted_iota(jnp.int32, (length, dim), 1)
    token = lax.broadcasted_iota(jnp.int32, (length, own), 0)
    turn_key = start_ref[0] + lax.broadcasted_iota(jnp.int32, (length, own), 1)
    visible = turn_key <= token

    def scores(head, s_ref):
        query = q_ref[:, head * dim : (head + 1) * dim]
        peak = None
        for c in range(chunks):
            keys = kv_ref[c * per_chunk : (c + 1) * per_chunk, 0:kv_rows, :].reshape(keys_at_once, dim)
            s = lax.dot_general(query, keys, contract, preferred_element_type=F32)
            s_ref[:, c * keys_at_once : (c + 1) * keys_at_once] = s
            for i in range(keys_at_once // dim):
                part = s[:, i * dim : (i + 1) * dim]
                peak = part if peak is None else jnp.maximum(peak, part)
        recent = lax.dot_general(query, tk_ref[...], contract, preferred_element_type=F32)
        recent = jnp.where(visible, recent, -jnp.inf)
        top = jnp.maximum(
            jnp.max(peak, axis=1, keepdims=True), jnp.max(recent, axis=1, keepdims=True)
        )
        shift = (top * log_factor).astype(BF16).astype(F32)
        return recent, shift

    def weights(head, s_ref, recent, shift):
        e = jnp.exp2(recent * log_factor - shift)
        total = jnp.sum(e, axis=1, keepdims=True)
        mixed = jnp.dot(e.astype(BF16), tv_ref[...], preferred_element_type=F32)
        spread = jnp.broadcast_to(shift, (length, dim))
        sums = None
        for c in range(chunks):
            values = kv_ref[c * per_chunk : (c + 1) * per_chunk, kv_rows : 2 * kv_rows, :].reshape(
                keys_at_once, dim
            )
            parts = []
            for i in range(keys_at_once // dim):
                at = c * keys_at_once + i * dim
                part = jnp.exp2(s_ref[:, at : at + dim] * log_factor - spread)
                sums = part if sums is None else sums + part
                parts.append(part.astype(BF16))
            mixed = mixed + jnp.dot(
                jnp.concatenate(parts, axis=1), values, preferred_element_type=F32
            )
        total = total + jnp.sum(sums, axis=1, keepdims=True)
        high = total.astype(BF16).astype(F32)
        stat = stat_ref[...]
        stat = jnp.where(lane == head, shift, stat)
        stat = jnp.where(lane == heads + head, high, stat)
        stat = jnp.where(lane == 2 * heads + head, total - high, stat)
        stat_ref[...] = stat
        msg_ref[:, head * own : (head + 1) * own, :] = mixed.astype(BF16).reshape(
            peers, own, dim
        )

    stat_ref[...] = jnp.zeros((length, dim), F32)
    held = scores(0, s_even)
    for head in range(heads):
        now, later = (s_even, s_odd) if head % 2 == 0 else (s_odd, s_even)
        coming = scores(head + 1, later) if head + 1 < heads else None
        weights(head, now, *held)
        held = coming
    msg_ref[:, heads * own :, :] = stat_ref[...].astype(BF16).reshape(peers, own, dim)


def combine_kernel(msg_ref, out_ref, *, heads):
    peers, _, dim = msg_ref.shape
    own = out_ref.shape[0]
    stats = [msg_ref[p, heads * own : (heads + 1) * own, :].astype(F32) for p in range(peers)]
    top = stats[0]
    for p in range(1, peers):
        top = jnp.maximum(top, stats[p])
    lane = lax.broadcasted_iota(jnp.int32, (own, dim), 1)
    keep = lane < heads
    factors, total = [], jnp.zeros((own, dim), F32)
    for p in range(peers):
        w = jnp.exp2(jnp.where(keep, stats[p] - top, 0.0))
        sums = pltpu.roll(stats[p], dim - heads, 1) + pltpu.roll(stats[p], dim - 2 * heads, 1)
        total = total + w * sums
        factors.append(w)
    total = jnp.where(keep, total, 1.0)
    factors = [w / total for w in factors]
    for h in range(heads):
        acc = None
        for p in range(peers):
            part = msg_ref[p, h * own : (h + 1) * own, :].astype(F32) * factors[p][:, h : h + 1]
            acc = part if acc is None else acc + part
        out_ref[:, h * dim : (h + 1) * dim] = acc.astype(BF16)


def whole(memory_space=pltpu.VMEM):
    return pl.BlockSpec(memory_space=memory_space)


def step(q_turn, k_turn, v_turn, cache_k, cache_v, k_scale, v_scale, page_map):
    peers = lax.axis_size("ctx")
    groups = lax.axis_size("head")
    position = lax.axis_index("ctx")
    slots, page_rows, dim = cache_k.shape
    half = slots // 2
    tokens = q_turn.shape[0]
    width = q_turn.shape[1] // groups
    heads = width // dim
    smem = whole(pltpu.SMEM)
    vmem = whole()

    turn = jnp.concatenate(
        [a.reshape(tokens, groups, -1) for a in (q_turn, k_turn, v_turn)], axis=2
    )
    turn = lax.all_to_all(turn, "head", split_axis=1, concat_axis=0, tiled=True)
    own = tokens * groups
    turn = turn.reshape(own, width + 2 * dim)
    q_mine = turn[:, :width]
    k_mine = turn[:, width : width + dim]
    v_mine = turn[:, width + dim :]

    queries = lax.all_gather(q_mine, "ctx", axis=0, tiled=True)
    length = queries.shape[0]

    send = pl.pallas_call(
        lambda *refs: prepare_kernel(*refs, half=half, peers=peers),
        out_shape=jax.ShapeDtypeStruct((peers, 4 * page_rows + INFO_ROWS, dim), BF16),
        in_specs=[smem, smem, smem, vmem, vmem],
        out_specs=vmem,
        name="prepare",
    )(page_map, k_scale.reshape(slots), v_scale.reshape(slots), cache_k, cache_v)
    queries, outgoing = lax.optimization_barrier((queries, send))
    recv = lax.all_to_all(outgoing, "ctx", split_axis=0, concat_axis=0, tiled=True)

    keys_at_once = 512
    attend = pl.pallas_call(
        lambda *refs: attend_kernel(*refs, factor=1.0 / math.sqrt(dim), keys_at_once=keys_at_once),
        out_shape=jax.ShapeDtypeStruct((peers, (heads + 1) * own, dim), BF16),
        in_specs=[smem, vmem, vmem, vmem, vmem],
        out_specs=vmem,
        scratch_shapes=[
            pltpu.VMEM((length, slots * page_rows), F32),
            pltpu.VMEM((length, slots * page_rows), F32),
            pltpu.VMEM((length, dim), F32),
        ],
        name="attend",
    )
    start = (position * own).reshape(1).astype(jnp.int32)
    msg = attend(start, queries, send, k_mine, v_mine)
    msg, recv = lax.optimization_barrier((msg, recv))
    parts = lax.all_to_all(msg, "ctx", split_axis=0, concat_axis=0, tiled=True)

    info = recv[:, 4 * page_rows : 4 * page_rows + 2, 0].astype(jnp.int32).reshape(2 * peers)
    paired = jax.ShapeDtypeStruct((slots * page_rows, dim), BF16)
    paired_k, paired_v = pl.pallas_call(
        lambda *refs: place_kernel(*refs, half=half, page_rows=page_rows),
        out_shape=(paired, paired),
        in_specs=[smem, vmem],
        out_specs=(vmem, vmem),
        name="place",
    )(info, recv)
    attn_out = pl.pallas_call(
        lambda *refs: combine_kernel(*refs, heads=heads),
        out_shape=jax.ShapeDtypeStruct((own, width), BF16),
        in_specs=[vmem],
        out_specs=vmem,
        name="combine",
    )(parts)
    return (attn_out, paired_k, paired_v)


def solution(mesh):
    return jax.shard_map(
        step,
        mesh=mesh,
        in_specs=(
            P(("rep", "ctx", "head"), None),
            P(("rep", "ctx", "head"), None),
            P(("rep", "ctx", "head"), None),
            P(("rep", "ctx"), None, "head"),
            P(("rep", "ctx"), None, "head"),
            P(("rep", "ctx"), "head"),
            P(("rep", "ctx"), "head"),
            P(("rep", "ctx")),
        ),
        out_specs=(P(("rep", "ctx"), "head"), P(("rep", "ctx"), "head"), P(("rep", "ctx"), "head")),
        check_vma=False,
    )
```

profile of v0, /device:TPU:1, one launch (start us, length us, event | category | flops | bytes accessed | tf_op | source)
XLA Modules:
  0.0 100.4 jit_solution(10209112235644621730)
XLA Ops:
  0.6 1.4 %pad_maximum_fusion = bf16[2,8,1280]{2,0,1:T(2,128)(2,1)} fusion(bf16[2,8,128]{2,0,1:T(2,128)(2,1)} %bitcast.13, bf16[2,8,128]{2,0,1:T(2,128)(2,1)} %bitcast.14, bf16[2,8,1024]{2,0,1:T(2,128)(2,1)} %bitcast.12), kind=kLoop, calls=%fused_computation | loop fusion | flops 122880 | bytes 81920 | tf_op jit(solution)/shard_map/concatenate | solution.py:177
  2.1 10.9 %all-to-all-start = ((bf16[2,8,1280]{2,0,1:T(2,128)(2,1)}), bf16[2,8,1280]{2,0,1:T(2,128)(2,1)S(1)}, u32[]{:S(2)}, u32[]{:S(2)}) async-start(bf16[2,8,1280]{2,0,1:T(2,128)(2,1)} %pad_maximum_fusion), calls=%async_computation | async-start | bytes 81920 | tf_op jit(solution)/shard_map/all_to_all | solution.py:180
  12.9 2.8 %prepare.1.refs_2_ = bf16[16,264,128]{2,1,0:T(8,128)(2,1)} custom-call(s32[32]{0:T(128)} %refs_0_.1, f32[32]{0:T(128)} %bitcast.15, f32[32]{0:T(128)} %bitcast.16, bf16[32,64,128]{2,1,0:T(8,128)(2,1)} %refs_3_.1, bf16[32,64,128]{2,1,0:T(8,128)(2,1)} %refs_4_.1), custom_call_target="tpu_custom_call" | custom-call | tf_op jit(solution)/shard_map/prepare/pallas_call | solution.py:190
  15.8 4.1 %all-to-all-done = bf16[2,8,1280]{2,0,1:T(2,128)(2,1)S(1)} async-done(((bf16[2,8,1280]{2,0,1:T(2,128)(2,1)}), bf16[2,8,1280]{2,0,1:T(2,128)(2,1)S(1)}, u32[]{:S(2)}, u32[]{:S(2)}) %all-to-all-start) | async-done | bytes 40992 | tf_op jit(solution)/shard_map/all_to_all | solution.py:180
  19.9 22.4 %all_gather.3.refs_1_ = bf16[256,1024]{1,0:T(8,128)(2,1)} all-gather(bf16[16,1024]{1,0:T(8,128)(2,1)S(1)} %slice.16), channel_id=1, replica_groups=mesh['ctx'=16,'head'=8,'rep'=4] {'ctx'}, dimensions={0}, use_global_device_ids=true | all-gather | bytes 557056 | tf_op jit(solution)/shard_map/all_gather | solution.py:187
  42.3 4.5 %all-to-all-start.1 = ((bf16[16,264,128]{2,1,0:T(8,128)(2,1)}), bf16[16,264,128]{2,1,0:T(8,128)(2,1)S(1)}, u32[]{:S(2)}, u32[]{:S(2)}) async-start(bf16[16,264,128]{2,1,0:T(8,128)(2,1)} %prepare.1.refs_2_), calls=%async_computation.1 | async-start | bytes 2162688 | tf_op jit(solution)/shard_map/all_to_all | solution.py:198
  46.8 0.6 fusion
  47.4 8.4 %attend.1 = bf16[16,144,128]{2,1,0:T(8,128)(2,1)} custom-call(s32[1]{0:T(128)} %bitcast.refs_0_, bf16[256,1024]{1,0:T(8,128)(2,1)} %all_gather.3.refs_1_, bf16[16,264,128]{2,1,0:T(8,128)(2,1)} %prepare.1.refs_2_, bf16[16,128]{1,0:T(8,128)(2,1)} %get-tuple-element.16.refs_3_, bf16[16,128]{1,0:T(8,128)(2,1)} %get-tuple-element.15.refs_4_), custom_call_target="tpu_custom_call" | custom-call | tf_op jit(solution)/shard_map/attend/pallas_call | solution.py:214
  55.8 19.6 %all-to-all-done.1.refs_1_ = bf16[16,264,128]{2,1,0:T(8,128)(2,1)S(1)} async-done(((bf16[16,264,128]{2,1,0:T(8,128)(2,1)}), bf16[16,264,128]{2,1,0:T(8,128)(2,1)S(1)}, u32[]{:S(2)}, u32[]{:S(2)}) %all-to-all-start.1) | async-done | bytes 1081376 | tf_op jit(solution)/shard_map/all_to_all | solution.py:198
  75.4 0.0 copy-start
  75.4 3.5 %all-to-all-start.2 = ((bf16[16,144,128]{2,1,0:T(8,128)(2,1)}), bf16[16,144,128]{2,1,0:T(8,128)(2,1)S(1)}, u32[]{:S(2)}, u32[]{:S(2)}) async-start(bf16[16,144,128]{2,1,0:T(8,128)(2,1)} %attend.1), calls=%async_computation.2 | async-start | bytes 1179648 | tf_op jit(solution)/shard_map/all_to_all | solution.py:216
  78.9 0.3 convert_reduce_fusion
  79.3 0.6 reshape.39.refs_0_
  79.9 0.0 copy-done
  79.9 2.4 %place.1 = (bf16[2048,128]{1,0:T(8,128)(2,1)}, bf16[2048,128]{1,0:T(8,128)(2,1)}) custom-call(s32[32]{0:T(128)} %reshape.39.refs_0_, bf16[16,264,128]{2,1,0:T(8,128)(2,1)} %copy-done), custom_call_target="tpu_custom_call" | custom-call | tf_op jit(solution)/shard_map/place/pallas_call | solution.py:220
  82.3 15.2 %all-to-all-done.2.refs_0_ = bf16[16,144,128]{2,1,0:T(8,128)(2,1)S(1)} async-done(((bf16[16,144,128]{2,1,0:T(8,128)(2,1)}), bf16[16,144,128]{2,1,0:T(8,128)(2,1)S(1)}, u32[]{:S(2)}, u32[]{:S(2)}) %all-to-all-start.2) | async-done | bytes 589856 | tf_op jit(solution)/shard_map/all_to_all | solution.py:216
  97.4 0.0 copy-start.1
  97.4 0.8 copy-done.1
  98.3 2.1 %combine.1 = bf16[16,1024]{1,0:T(8,128)(2,1)} custom-call(bf16[16,144,128]{2,1,0:T(8,128)(2,1)} %copy-done.1), custom_call_target="tpu_custom_call" | custom-call | tf_op jit(solution)/shard_map/combine/pallas_call | solution.py:227
  (2 shorter events, 0.0 us)
Async XLA Ops:
  2.1 17.8 %all-to-all-start = ((bf16[2,8,1280]{2,0,1:T(2,128)(2,1)}), bf16[2,8,1280]{2,0,1:T(2,128)(2,1)S(1)}, u32[]{:S(2)}, u32[]{:S(2)}) async-start(bf16[2,8,1280]{2,0,1:T(2,128)(2,1)} %pad_maximum_fusion), calls=%async_computation | async-start | bytes 81920 | tf_op jit(solution)/shard_map/all_to_all | solution.py:180
  42.3 33.1 %all-to-all-start.1 = ((bf16[16,264,128]{2,1,0:T(8,128)(2,1)}), bf16[16,264,128]{2,1,0:T(8,128)(2,1)S(1)}, u32[]{:S(2)}, u32[]{:S(2)}) async-start(bf16[16,264,128]{2,1,0:T(8,128)(2,1)} %prepare.1.refs_2_), calls=%async_computation.1 | async-start | bytes 2162688 | tf_op jit(solution)/shard_map/all_to_all | solution.py:198
  75.4 4.4 %copy-start = (bf16[16,264,128]{2,1,0:T(8,128)(2,1)}, bf16[16,264,128]{2,1,0:T(8,128)(2,1)S(1)}, u32[]{:S(2)}) copy-start(bf16[16,264,128]{2,1,0:T(8,128)(2,1)S(1)} %all-to-all-done.1.refs_1_) | copy-start | bytes 3244036
  75.4 22.0 %all-to-all-start.2 = ((bf16[16,144,128]{2,1,0:T(8,128)(2,1)}), bf16[16,144,128]{2,1,0:T(8,128)(2,1)S(1)}, u32[]{:S(2)}, u32[]{:S(2)}) async-start(bf16[16,144,128]{2,1,0:T(8,128)(2,1)} %attend.1), calls=%async_computation.2 | async-start | bytes 1179648 | tf_op jit(solution)/shard_map/all_to_all | solution.py:216
  97.4 0.8 copy-start.1
where the time goes:
time: 101 us; the launch traced here: 100 us
  waiting for transfers between devices  38.9 us (39%)
  blocking collectives  22.4 us (22%)
  starting transfers between devices  18.8 us (19%)
  Pallas kernels  15.8 us (16%)
  local copies, waits for them, and re-layouts  2.04 us (2%)
  other arithmetic  1.79 us (2%)
    all_gather x1, blocking collectives, step(): queries = lax.all_gather(q_mine, 'ctx', axis=0, tiled=True)  22.4 us
    all_to_all x1, waiting for transfers between devices, step(): lax.all_to_all(outgoing, 'ctx', split_axis=0, concat_axis=0, tiled=True)  19.6 us
    all_to_all x1, waiting for transfers between devices, step(): parts = lax.all_to_all(msg, 'ctx', split_axis=0, concat_axis=0, tiled=True)  15.2 us
    all_to_all x1, starting transfers between devices, step(): turn = lax.all_to_all(turn, 'head', split_axis=1, concat_axis=0, tiled=True)  10.9 us
    pallas_call x1, Pallas kernels, step(): msg = attend(start, queries, send, k_mine, v_mine)  8.42 us
    all_to_all x1, starting transfers between devices, step(): lax.all_to_all(outgoing, 'ctx', split_axis=0, concat_axis=0, tiled=True)  4.49 us
    all_to_all x1, waiting for transfers between devices, step(): turn = lax.all_to_all(turn, 'head', split_axis=1, concat_axis=0, tiled=True)  4.12 us
    all_to_all x1, starting transfers between devices, step(): parts = lax.all_to_all(msg, 'ctx', split_axis=0, concat_axis=0, tiled=True)  3.48 us
  transfers between devices with their start and end apart: 3, of which 3 were waited for; matrix products, arithmetic and copies ran while one was open for 2% of the time, Pallas kernels for 14%

commit v1 on v0

--- a/solution.py
+++ b/solution.py
@@ -8,9 +8,25 @@
 from jax.sharding import PartitionSpec as P
 
 
-INFO_ROWS = 8
+INFO_ROWS = 16
+CORES = 2
 BF16 = jnp.bfloat16
 F32 = jnp.float32
+
+
+def pack_kernel(q_ref, k_ref, v_ref, out_ref, *, groups):
+    dim = k_ref.shape[1] // groups
+    share = q_ref.shape[1] // (groups * CORES)
+    for group in range(groups):
+        keys = k_ref[:, group * dim : (group + 1) * dim]
+        values = v_ref[:, group * dim : (group + 1) * dim]
+        for core in range(CORES):
+            at = (group * CORES + core) * share
+            query = q_ref[:, at : at + share]
+            for to in range(core * groups + group, out_ref.shape[0], CORES * groups):
+                out_ref[to, :, :share] = query
+                out_ref[to, :, share : share + dim] = keys
+                out_ref[to, :, share + dim :] = values
 
 
 def prepare_kernel(map_ref, k_scale_ref, v_scale_ref, k_ref, v_ref, send_ref, *, half, peers):
@@ -59,33 +75,41 @@
 
 
 def attend_kernel(
-    start_ref, q_ref, kv_ref, tk_ref, tv_ref, msg_ref, s_even, s_odd, stat_ref, *, factor, keys_at_once
+    start_ref, turn_ref, kv_ref, other_ref, msg_ref, s_even, s_odd, stat_ref, *, factor, keys_at_once
 ):
     peers, _, dim = kv_ref.shape
-    length, width = q_ref.shape
-    heads = width // dim
-    own = tk_ref.shape[0]
+    length, width = turn_ref.shape
+    heads = width // dim - 2
+    own = length // peers
+    recent_keys = CORES * own
     kv_rows = (kv_ref.shape[1] - INFO_ROWS) // 2
     per_chunk = keys_at_once // kv_rows
-    chunks = peers // per_chunk
+    places = [(ref, c) for ref in (kv_ref, other_ref) for c in range(peers // per_chunk)]
     log_factor = factor * math.log2(math.e)
     contract = (((1,), (1,)), ((), ()))
+    start = pl.multiple_of(start_ref[0], recent_keys)
+    turn_k = turn_ref[pl.ds(start, recent_keys), heads * dim : (heads + 1) * dim]
+    turn_v = turn_ref[pl.ds(start, recent_keys), (heads + 1) * dim : (heads + 2) * dim]
     lane = lax.broadcasted_iota(jnp.int32, (length, dim), 1)
-    token = lax.broadcasted_iota(jnp.int32, (length, own), 0)
-    turn_key = start_ref[0] + lax.broadcasted_iota(jnp.int32, (length, own), 1)
+    token = lax.broadcasted_iota(jnp.int32, (length, recent_keys), 0)
+    turn_key = start + lax.broadcasted_iota(jnp.int32, (length, recent_keys), 1)
     visible = turn_key <= token
 
+    def chunk(place, first_row):
+        ref, c = place
+        rows = ref[c * per_chunk : (c + 1) * per_chunk, first_row : first_row + kv_rows, :]
+        return rows.reshape(keys_at_once, dim)
+
     def scores(head, s_ref):
-        query = q_ref[:, head * dim : (head + 1) * dim]
+        query = turn_ref[:, head * dim : (head + 1) * dim]
         peak = None
-        for c in range(chunks):
-            keys = kv_ref[c * per_chunk : (c + 1) * per_chunk, 0:kv_rows, :].reshape(keys_at_once, dim)
-            s = lax.dot_general(query, keys, contract, preferred_element_type=F32)
-            s_ref[:, c * keys_at_once : (c + 1) * keys_at_once] = s
+        for n, place in enumerate(places):
+            s = lax.dot_general(query, chunk(place, 0), contract, preferred_element_type=F32)
+            s_ref[:, n * keys_at_once : (n + 1) * keys_at_once] = s
             for i in range(keys_at_once // dim):
                 part = s[:, i * dim : (i + 1) * dim]
                 peak = part if peak is None else jnp.maximum(peak, part)
-        recent = lax.dot_general(query, tk_ref[...], contract, preferred_element_type=F32)
+        recent = lax.dot_general(query, turn_k, contract, preferred_element_type=F32)
         recent = jnp.where(visible, recent, -jnp.inf)
         top = jnp.maximum(
             jnp.max(peak, axis=1, keepdims=True), jnp.max(recent, axis=1, keepdims=True)
@@ -96,21 +120,18 @@
     def weights(head, s_ref, recent, shift):
         e = jnp.exp2(recent * log_factor - shift)
         total = jnp.sum(e, axis=1, keepdims=True)
-        mixed = jnp.dot(e.astype(BF16), tv_ref[...], preferred_element_type=F32)
+        mixed = jnp.dot(e.astype(BF16), turn_v, preferred_element_type=F32)
         spread = jnp.broadcast_to(shift, (length, dim))
         sums = None
-        for c in range(chunks):
-            values = kv_ref[c * per_chunk : (c + 1) * per_chunk, kv_rows : 2 * kv_rows, :].reshape(
-                keys_at_once, dim
-            )
+        for n, place in enumerate(places):
             parts = []
             for i in range(keys_at_once // dim):
-                at = c * keys_at_once + i * dim
+                at = n * keys_at_once + i * dim
                 part = jnp.exp2(s_ref[:, at : at + dim] * log_factor - spread)
                 sums = part if sums is None else sums + part
                 parts.append(part.astype(BF16))
             mixed = mixed + jnp.dot(
-                jnp.concatenate(parts, axis=1), values, preferred_element_type=F32
+                jnp.concatenate(parts, axis=1), chunk(place, kv_rows), preferred_element_type=F32
             )
         total = total + jnp.sum(sums, axis=1, keepdims=True)
         high = total.astype(BF16).astype(F32)
@@ -133,29 +154,32 @@
     msg_ref[:, heads * own :, :] = stat_ref[...].astype(BF16).reshape(peers, own, dim)
 
 
-def combine_kernel(msg_ref, out_ref, *, heads):
-    peers, _, dim = msg_ref.shape
+def combine_kernel(msg_ref, out_ref):
+    peers, rows, dim = msg_ref.shape
     own = out_ref.shape[0]
-    stats = [msg_ref[p, heads * own : (heads + 1) * own, :].astype(F32) for p in range(peers)]
-    top = stats[0]
-    for p in range(1, peers):
-        top = jnp.maximum(top, stats[p])
-    lane = lax.broadcasted_iota(jnp.int32, (own, dim), 1)
-    keep = lane < heads
-    factors, total = [], jnp.zeros((own, dim), F32)
-    for p in range(peers):
-        w = jnp.exp2(jnp.where(keep, stats[p] - top, 0.0))
-        sums = pltpu.roll(stats[p], dim - heads, 1) + pltpu.roll(stats[p], dim - 2 * heads, 1)
-        total = total + w * sums
-        factors.append(w)
-    total = jnp.where(keep, total, 1.0)
-    factors = [w / total for w in factors]
-    for h in range(heads):
-        acc = None
-        for p in range(peers):
-            part = msg_ref[p, h * own : (h + 1) * own, :].astype(F32) * factors[p][:, h : h + 1]
-            acc = part if acc is None else acc + part
-        out_ref[:, h * dim : (h + 1) * dim] = acc.astype(BF16)
+    heads = rows // own - 1
+    keep = lax.broadcasted_iota(jnp.int32, (own, dim), 1) < heads
+    for share in range(CORES):
+        senders = range(share, peers, CORES)
+        stats = [msg_ref[p, heads * own :, :].astype(F32) for p in senders]
+        top = stats[0]
+        for stat in stats[1:]:
+            top = jnp.maximum(top, stat)
+        factors, total = [], jnp.zeros((own, dim), F32)
+        for stat in stats:
+            w = jnp.exp2(jnp.where(keep, stat - top, 0.0))
+            sums = pltpu.roll(stat, dim - heads, 1) + pltpu.roll(stat, dim - 2 * heads, 1)
+            total = total + w * sums
+            factors.append(w)
+        total = jnp.where(keep, total, 1.0)
+        factors = [w / total for w in factors]
+        for h in range(heads):
+            acc = None
+            for p, w in zip(senders, factors):
+                part = msg_ref[p, h * own : (h + 1) * own, :].astype(F32) * w[:, h : h + 1]
+                acc = part if acc is None else acc + part
+            at = (share * heads + h) * dim
+            out_ref[:, at : at + dim] = acc.astype(BF16)
 
 
 def whole(memory_space=pltpu.VMEM):
@@ -169,49 +193,50 @@
     slots, page_rows, dim = cache_k.shape
     half = slots // 2
     tokens = q_turn.shape[0]
+    own = tokens * groups
+    length = own * peers
     width = q_turn.shape[1] // groups
-    heads = width // dim
+    share = width // CORES
+    heads = share // dim
     smem = whole(pltpu.SMEM)
     vmem = whole()
 
-    turn = jnp.concatenate(
-        [a.reshape(tokens, groups, -1) for a in (q_turn, k_turn, v_turn)], axis=2
-    )
-    turn = lax.all_to_all(turn, "head", split_axis=1, concat_axis=0, tiled=True)
-    own = tokens * groups
-    turn = turn.reshape(own, width + 2 * dim)
-    q_mine = turn[:, :width]
-    k_mine = turn[:, width : width + dim]
-    v_mine = turn[:, width + dim :]
-
-    queries = lax.all_gather(q_mine, "ctx", axis=0, tiled=True)
-    length = queries.shape[0]
-
-    send = pl.pallas_call(
+    turn = pl.pallas_call(
+        lambda *refs: pack_kernel(*refs, groups=groups),
+        out_shape=jax.ShapeDtypeStruct((peers * groups, tokens, share + 2 * dim), BF16),
+        in_specs=[vmem, vmem, vmem],
+        out_specs=vmem,
+        name="pack",
+    )(q_turn, k_turn, v_turn)
+    turn = lax.all_to_all(turn, ("ctx", "head"), split_axis=0, concat_axis=0, tiled=True)
+
+    prepare = pl.pallas_call(
         lambda *refs: prepare_kernel(*refs, half=half, peers=peers),
         out_shape=jax.ShapeDtypeStruct((peers, 4 * page_rows + INFO_ROWS, dim), BF16),
         in_specs=[smem, smem, smem, vmem, vmem],
         out_specs=vmem,
         name="prepare",
-    )(page_map, k_scale.reshape(slots), v_scale.reshape(slots), cache_k, cache_v)
-    queries, outgoing = lax.optimization_barrier((queries, send))
+    )
+    send = prepare(page_map, k_scale.reshape(slots), v_scale.reshape(slots), cache_k, cache_v)
+    other = lax.ppermute(send, "ctx", [(i, i ^ 1) for i in range(peers)])
+    turn, other, outgoing = lax.optimization_barrier((turn, other, send))
+    turn = turn.reshape(length, share + 2 * dim)
     recv = lax.all_to_all(outgoing, "ctx", split_axis=0, concat_axis=0, tiled=True)
 
-    keys_at_once = 512
     attend = pl.pallas_call(
-        lambda *refs: attend_kernel(*refs, factor=1.0 / math.sqrt(dim), keys_at_once=keys_at_once),
+        lambda *refs: attend_kernel(*refs, factor=1.0 / math.sqrt(dim), keys_at_once=512),
         out_shape=jax.ShapeDtypeStruct((peers, (heads + 1) * own, dim), BF16),
-        in_specs=[smem, vmem, vmem, vmem, vmem],
+        in_specs=[smem, vmem, vmem, vmem],
         out_specs=vmem,
         scratch_shapes=[
-            pltpu.VMEM((length, slots * page_rows), F32),
-            pltpu.VMEM((length, slots * page_rows), F32),
+            pltpu.VMEM((length, CORES * slots * page_rows), F32),
+            pltpu.VMEM((length, CORES * slots * page_rows), F32),
             pltpu.VMEM((length, dim), F32),
         ],
         name="attend",
     )
-    start = (position * own).reshape(1).astype(jnp.int32)
-    msg = attend(start, queries, send, k_mine, v_mine)
+    start = (position // CORES * (CORES * own)).reshape(1).astype(jnp.int32)
+    msg = attend(start, turn, send, other)
     msg, recv = lax.optimization_barrier((msg, recv))
     parts = lax.all_to_all(msg, "ctx", split_axis=0, concat_axis=0, tiled=True)
 
@@ -225,7 +250,7 @@
         name="place",
     )(info, recv)
     attn_out = pl.pallas_call(
-        lambda *refs: combine_kernel(*refs, heads=heads),
+        combine_kernel,
         out_shape=jax.ShapeDtypeStruct((own, width), BF16),
         in_specs=[vmem],
         out_specs=vmem,

time: 101 us -> 96.4 us (0.954)
  waiting for transfers between devices: 38.9 us -> 28.7 us
  blocking collectives: 22.4 us -> 29.8 us
  starting transfers between devices: 18.8 us -> 15.8 us
  Pallas kernels: 15.8 us -> 18.2 us
  other arithmetic: 1.79 us -> 0.34 us
    all_to_all x0 -> x1, blocking collectives: none -> 29.8 us  [step(): lax.all_to_all(turn, ('ctx', 'head'), split_axis=0, concat_axis=0, tiled=...]
    all_gather x1 -> x0, blocking collectives: 22.4 us -> none  [step(): queries = lax.all_gather(q_mine, 'ctx', axis=0, tiled=True)]
    all_to_all x1 -> x0, starting transfers between devices: 10.9 us -> none  [step(): turn = lax.all_to_all(turn, 'head', split_axis=1, concat_axis=0, tiled=True)]
    ppermute x0 -> x1, starting transfers between devices: none -> 8.73 us  [step(): other = lax.ppermute(send, 'ctx', [(i, i ^ 1) for i in range(peers)])]
    all_to_all x1, waiting for transfers between devices: 15.2 us -> 9.61 us  [step(): parts = lax.all_to_all(msg, 'ctx', split_axis=0, concat_axis=0, tiled=True)]
    all_to_all x1 -> x0, waiting for transfers between devices: 4.12 us -> none  [step(): turn = lax.all_to_all(turn, 'head', split_axis=1, concat_axis=0, tiled=True)]
    pallas_call x3 -> x4, Pallas kernels: 13.4 us -> 15.8 us  [the longest x1 9.27 us: step(): msg = attend(start, turn, send, other)]
    concatenate x1 -> x0, other arithmetic: 1.45 us -> none  [step(): jnp.concatenate([a.reshape(tokens, groups, -1) for a in (q_turn, k_turn,...]
  transfers between devices with their start and end apart: 3 -> 3, of which waited for: 3 -> 2; matrix products, arithmetic and copies ran while one was open for 2% -> 2% of each run, Pallas kernels for 14% -> 14%
where the time goes in v1:
time: 96.4 us; the launch traced here: 95.8 us
  blocking collectives  29.8 us (31%)
  waiting for transfers between devices  28.7 us (30%)
  Pallas kernels  18.2 us (19%)
  starting transfers between devices  15.8 us (16%)
  local copies, waits for them, and re-layouts  2.25 us (2%)
    all_to_all x1, blocking collectives, step(): lax.all_to_all(turn, ('ctx', 'head'), split_axis=0, concat_axis=0, tiled=...  29.8 us
    all_to_all x1, waiting for transfers between devices, step(): lax.all_to_all(outgoing, 'ctx', split_axis=0, concat_axis=0, tiled=True)  19.1 us
    all_to_all x1, waiting for transfers between devices, step(): parts = lax.all_to_all(msg, 'ctx', split_axis=0, concat_axis=0, tiled=True)  9.61 us
    pallas_call x1, Pallas kernels, step(): msg = attend(start, turn, send, other)  9.27 us
    ppermute x1, starting transfers between devices, step(): other = lax.ppermute(send, 'ctx', [(i, i ^ 1) for i in range(peers)])  8.73 us
    all_to_all x1, starting transfers between devices, step(): lax.all_to_all(outgoing, 'ctx', split_axis=0, concat_axis=0, tiled=True)  3.6 us
    all_to_all x1, starting transfers between devices, step(): parts = lax.all_to_all(msg, 'ctx', split_axis=0, concat_axis=0, tiled=True)  3.52 us
    pallas_call x1, Pallas kernels, step(): prepare(page_map, k_scale.reshape(slots), v_scale.reshape(slots), cache_k...  2.88 us
  transfers between devices with their start and end apart: 3, of which 2 were waited for; matrix products, arithmetic and copies ran while one was open for 2% of the time, Pallas kernels for 14%

profile of v1, /device:TPU:1, one launch (start us, length us, event | category | flops | bytes accessed | tf_op | source)
XLA Modules:
  0.0 95.8 jit_solution(9739357346668709643)
XLA Ops:
  0.6 2.9 %prepare.1.refs_2_ = bf16[16,272,128]{2,1,0:T(8,128)(2,1)} custom-call(s32[32]{0:T(128)} %refs_0_.3, f32[32]{0:T(128)} %bitcast.3, f32[32]{0:T(128)} %bitcast.4, bf16[32,64,128]{2,1,0:T(8,128)(2,1)} %refs_3_.1, bf16[32,64,128]{2,1,0:T(8,128)(2,1)} %refs_4_.1), custom_call_target="tpu_custom_call" | custom-call | tf_op jit(solution)/shard_map/prepare/pallas_call | solution.py:220
  3.5 8.7 %collective-permute-start = (bf16[16,272,128]{2,1,0:T(8,128)(2,1)}, bf16[16,272,128]{2,1,0:T(8,128)(2,1)S(1)}, u32[]{:S(2)}, u32[]{:S(2)}) collective-permute-start(bf16[16,272,128]{2,1,0:T(8,128)(2,1)} %prepare.1.refs_2_), channel_id=1, source_target_pairs={{0,32},{32,0},{64,96},{96,64},{128,160},{160,128},{192,224},{224,1... | collective-permute-start | bytes 3342344 | tf_op jit(solution)/shard_map/ppermute | solution.py:221
  12.3 1.6 %pack.1 = bf16[128,2,768]{2,1,0:T(2,128)(2,1)} custom-call(bf16[2,8192]{1,0:T(2,128)(2,1)} %refs_0_.2, bf16[2,1024]{1,0:T(2,128)(2,1)} %refs_1_.1, bf16[2,1024]{1,0:T(2,128)(2,1)} %refs_2_.1), custom_call_target="tpu_custom_call" | custom-call | tf_op jit(solution)/shard_map/pack/pallas_call | solution.py:204
  13.9 29.8 %all_to_all.15 = bf16[128,2,768]{2,1,0:T(2,128)(2,1)S(1)} all-to-all(bf16[128,2,768]{2,1,0:T(2,128)(2,1)} %pack.1), channel_id=1, replica_groups=mesh['ctx'=16,'head'=8,'rep'=4] {'ctx','head'}, dimensions={0} | all-to-all | bytes 786432 | tf_op jit(solution)/shard_map/all_to_all | solution.py:211
  43.7 0.0 collective-permute-done.refs_3_
  43.7 0.0 copy-start.2
  43.7 3.6 %all-to-all-start.1 = ((bf16[16,272,128]{2,1,0:T(8,128)(2,1)}), bf16[16,272,128]{2,1,0:T(8,128)(2,1)S(1)}, u32[]{:S(2)}, u32[]{:S(2)}) async-start(bf16[16,272,128]{2,1,0:T(8,128)(2,1)} %prepare.1.refs_2_), calls=%async_computation.1 | async-start | bytes 2228224 | tf_op jit(solution)/shard_map/all_to_all | solution.py:224
  47.3 0.0 copy-done.2
  47.3 0.9 reshape.25.refs_1_
  48.2 9.3 %attend.1 = bf16[16,80,128]{2,1,0:T(8,128)(2,1)} custom-call(s32[1]{0:T(128)} %bitcast.refs_0_, bf16[256,768]{1,0:T(8,128)(2,1)} %reshape.25.refs_1_, bf16[16,272,128]{2,1,0:T(8,128)(2,1)} %prepare.1.refs_2_, bf16[16,272,128]{2,1,0:T(8,128)(2,1)} %copy-done.2), custom_call_target="tpu_custom_call" | custom-call | tf_op jit(solution)/shard_map/attend/pallas_call | solution.py:239
  57.5 19.1 %all-to-all-done.1.refs_1_ = bf16[16,272,128]{2,1,0:T(8,128)(2,1)S(1)} async-done(((bf16[16,272,128]{2,1,0:T(8,128)(2,1)}), bf16[16,272,128]{2,1,0:T(8,128)(2,1)S(1)}, u32[]{:S(2)}, u32[]{:S(2)}) %all-to-all-start.1) | async-done | bytes 1114144 | tf_op jit(solution)/shard_map/all_to_all | solution.py:224
  76.6 0.0 copy-start
  76.6 3.5 %all-to-all-start.2 = ((bf16[16,80,128]{2,1,0:T(8,128)(2,1)}), bf16[16,80,128]{2,1,0:T(8,128)(2,1)S(1)}, u32[]{:S(2)}, u32[]{:S(2)}) async-start(bf16[16,80,128]{2,1,0:T(8,128)(2,1)} %attend.1), calls=%async_computation.2 | async-start | bytes 655360 | tf_op jit(solution)/shard_map/all_to_all | solution.py:241
  80.1 0.3 convert_reduce_fusion
  80.4 0.6 reshape.26.refs_0_
  81.1 0.0 copy-done
  81.1 2.4 %place.1 = (bf16[2048,128]{1,0:T(8,128)(2,1)}, bf16[2048,128]{1,0:T(8,128)(2,1)}) custom-call(s32[32]{0:T(128)} %reshape.26.refs_0_, bf16[16,272,128]{2,1,0:T(8,128)(2,1)} %copy-done), custom_call_target="tpu_custom_call" | custom-call | tf_op jit(solution)/shard_map/place/pallas_call | solution.py:245
  83.5 9.6 %all-to-all-done.2.msg_ref = bf16[16,80,128]{2,1,0:T(8,128)(2,1)S(1)} async-done(((bf16[16,80,128]{2,1,0:T(8,128)(2,1)}), bf16[16,80,128]{2,1,0:T(8,128)(2,1)S(1)}, u32[]{:S(2)}, u32[]{:S(2)}) %all-to-all-start.2) | async-done | bytes 327712 | tf_op jit(solution)/shard_map/all_to_all | solution.py:241
  93.1 0.0 copy-start.1
  93.1 0.7 copy-done.1
  93.8 2.0 %combine.1 = bf16[16,1024]{1,0:T(8,128)(2,1)} custom-call(bf16[16,80,128]{2,1,0:T(8,128)(2,1)} %copy-done.1), custom_call_target="tpu_custom_call" | custom-call | tf_op jit(solution)/shard_map/combine/pallas_call | solution.py:252
Async XLA Ops:
  3.5 40.2 %collective-permute-start = (bf16[16,272,128]{2,1,0:T(8,128)(2,1)}, bf16[16,272,128]{2,1,0:T(8,128)(2,1)S(1)}, u32[]{:S(2)}, u32[]{:S(2)}) collective-permute-start(bf16[16,272,128]{2,1,0:T(8,128)(2,1)} %prepare.1.refs_2_), channel_id=1, source_target_pairs={{0,32},{32,0},{64,96},{96,64},{128,160},{160,128},{192,224},{224,1... | collective-permute-start | bytes 3342344 | tf_op jit(solution)/shard_map/ppermute | solution.py:221
  43.7 3.6 %copy-start.2 = (bf16[16,272,128]{2,1,0:T(8,128)(2,1)}, bf16[16,272,128]{2,1,0:T(8,128)(2,1)S(1)}, u32[]{:S(2)}) copy-start(bf16[16,272,128]{2,1,0:T(8,128)(2,1)S(1)} %collective-permute-done.refs_3_) | copy-start | bytes 3342340
  43.7 32.9 %all-to-all-start.1 = ((bf16[16,272,128]{2,1,0:T(8,128)(2,1)}), bf16[16,272,128]{2,1,0:T(8,128)(2,1)S(1)}, u32[]{:S(2)}, u32[]{:S(2)}) async-start(bf16[16,272,128]{2,1,0:T(8,128)(2,1)} %prepare.1.refs_2_), calls=%async_computation.1 | async-start | bytes 2228224 | tf_op jit(solution)/shard_map/all_to_all | solution.py:224
  76.6 4.5 %copy-start = (bf16[16,272,128]{2,1,0:T(8,128)(2,1)}, bf16[16,272,128]{2,1,0:T(8,128)(2,1)S(1)}, u32[]{:S(2)}) copy-start(bf16[16,272,128]{2,1,0:T(8,128)(2,1)S(1)} %all-to-all-done.1.refs_1_) | copy-start | bytes 3342340
  76.6 16.5 %all-to-all-start.2 = ((bf16[16,80,128]{2,1,0:T(8,128)(2,1)}), bf16[16,80,128]{2,1,0:T(8,128)(2,1)S(1)}, u32[]{:S(2)}, u32[]{:S(2)}) async-start(bf16[16,80,128]{2,1,0:T(8,128)(2,1)} %attend.1), calls=%async_computation.2 | async-start | bytes 655360 | tf_op jit(solution)/shard_map/all_to_all | solution.py:241
  93.1 0.7 copy-start.1

commit v2 on v1

--- a/solution.py
+++ b/solution.py
@@ -12,6 +12,7 @@
 CORES = 2
 BF16 = jnp.bfloat16
 F32 = jnp.float32
+SMALL = pltpu.CompilerParams(vmem_limit_bytes=16 << 20)
 
 
 def pack_kernel(q_ref, k_ref, v_ref, out_ref, *, groups):
@@ -186,6 +187,10 @@
     return pl.BlockSpec(memory_space=memory_space)
 
 
+def near(x):
+    return pltpu.with_memory_space_constraint(x, pltpu.VMEM)
+
+
 def step(q_turn, k_turn, v_turn, cache_k, cache_v, k_scale, v_scale, page_map):
     peers = lax.axis_size("ctx")
     groups = lax.axis_size("head")
@@ -219,7 +224,7 @@
     )
     send = prepare(page_map, k_scale.reshape(slots), v_scale.reshape(slots), cache_k, cache_v)
     other = lax.ppermute(send, "ctx", [(i, i ^ 1) for i in range(peers)])
-    turn, other, outgoing = lax.optimization_barrier((turn, other, send))
+    turn, outgoing = lax.optimization_barrier((turn, send))
     turn = turn.reshape(length, share + 2 * dim)
     recv = lax.all_to_all(outgoing, "ctx", split_axis=0, concat_axis=0, tiled=True)
 
@@ -242,20 +247,23 @@
 
     info = recv[:, 4 * page_rows : 4 * page_rows + 2, 0].astype(jnp.int32).reshape(2 * peers)
     paired = jax.ShapeDtypeStruct((slots * page_rows, dim), BF16)
-    paired_k, paired_v = pl.pallas_call(
+    place = pl.pallas_call(
         lambda *refs: place_kernel(*refs, half=half, page_rows=page_rows),
         out_shape=(paired, paired),
         in_specs=[smem, vmem],
         out_specs=(vmem, vmem),
+        compiler_params=SMALL,
         name="place",
-    )(info, recv)
+    )
+    paired_k, paired_v = place(info, near(recv))
     attn_out = pl.pallas_call(
         combine_kernel,
         out_shape=jax.ShapeDtypeStruct((own, width), BF16),
         in_specs=[vmem],
         out_specs=vmem,
+        compiler_params=SMALL,
         name="combine",
-    )(parts)
+    )(near(parts))
     return (attn_out, paired_k, paired_v)
 
 

time: 96.4 us -> 89.7 us (0.930)
  blocking collectives: 29.8 us -> 0 us
  waiting for transfers between devices: 28.7 us -> 43.2 us
  starting transfers between devices: 15.8 us -> 27.5 us
  Pallas kernels: 18.2 us -> 16.5 us
  local copies, waits for them, and re-layouts: 2.25 us -> 0.99 us
    all_to_all x1 -> x0, blocking collectives: 29.8 us -> none  [step(): lax.all_to_all(turn, ('ctx', 'head'), split_axis=0, concat_axis=0, tiled=...]
    all_to_all x0 -> x1, starting transfers between devices: none -> 18.4 us  [step(): lax.all_to_all(turn, ('ctx', 'head'), split_axis=0, concat_axis=0, tiled=...]
    all_to_all x0 -> x1, waiting for transfers between devices: none -> 15.2 us  [step(): lax.all_to_all(turn, ('ctx', 'head'), split_axis=0, concat_axis=0, tiled=...]
    ppermute x1, starting transfers between devices: 8.73 us -> 1.98 us  [step(): other = lax.ppermute(send, 'ctx', [(i, i ^ 1) for i in range(peers)])]
    all_to_all x1, waiting for transfers between devices: 19.1 us -> 15.2 us  [step(): lax.all_to_all(outgoing, 'ctx', split_axis=0, concat_axis=0, tiled=True)]
    ppermute x1, waiting for transfers between devices: 0.01 us -> 1.88 us  [step(): other = lax.ppermute(send, 'ctx', [(i, i ^ 1) for i in range(peers)])]
    all_to_all x1, waiting for transfers between devices: 9.61 us -> 10.8 us  [step(): parts = lax.all_to_all(msg, 'ctx', split_axis=0, concat_axis=0, tiled=True)]
    pallas_call x1, Pallas kernels: 2.02 us -> 1.05 us  [step(): pl.pallas_call(combine_kernel, out_shape=jax.ShapeDtypeStruct((own, width...]
  transfers between devices with their start and end apart: 3 -> 4, of which waited for: 2 -> 4; matrix products, arithmetic and copies ran while one was open for 2% -> 1% of each run, Pallas kernels for 14% -> 16%
where the time goes in v2:
time: 89.7 us; the launch traced here: 89.2 us
  waiting for transfers between devices  43.2 us (48%)
  starting transfers between devices  27.5 us (31%)
  Pallas kernels  16.5 us (18%)
  local copies, waits for them, and re-layouts  0.99 us (1%)
    all_to_all x1, starting transfers between devices, step(): lax.all_to_all(turn, ('ctx', 'head'), split_axis=0, concat_axis=0, tiled=...  18.4 us
    all_to_all x1, waiting for transfers between devices, step(): lax.all_to_all(turn, ('ctx', 'head'), split_axis=0, concat_axis=0, tiled=...  15.2 us
    all_to_all x1, waiting for transfers between devices, step(): lax.all_to_all(outgoing, 'ctx', split_axis=0, concat_axis=0, tiled=True)  15.2 us
    all_to_all x1, waiting for transfers between devices, step(): parts = lax.all_to_all(msg, 'ctx', split_axis=0, concat_axis=0, tiled=True)  10.8 us
    pallas_call x1, Pallas kernels, step(): msg = attend(start, turn, send, other)  9.26 us
    all_to_all x1, starting transfers between devices, step(): lax.all_to_all(outgoing, 'ctx', split_axis=0, concat_axis=0, tiled=True)  3.59 us
    all_to_all x1, starting transfers between devices, step(): parts = lax.all_to_all(msg, 'ctx', split_axis=0, concat_axis=0, tiled=True)  3.52 us
    pallas_call x1, Pallas kernels, step(): prepare(page_map, k_scale.reshape(slots), v_scale.reshape(slots), cache_k...  2.88 us
  transfers between devices with their start and end apart: 4, of which 4 were waited for; matrix products, arithmetic and copies ran while one was open for 1% of the time, Pallas kernels for 16%

profile of v2, /device:TPU:1, one launch (start us, length us, event | category | flops | bytes accessed | tf_op | source)
XLA Modules:
  0.0 89.2 jit_solution(9383881260684005297)
XLA Ops:
  0.6 1.6 %pack.1 = bf16[128,2,768]{2,1,0:T(2,128)(2,1)} custom-call(bf16[2,8192]{1,0:T(2,128)(2,1)} %refs_0_.2, bf16[2,1024]{1,0:T(2,128)(2,1)} %refs_1_.1, bf16[2,1024]{1,0:T(2,128)(2,1)} %refs_2_.1), custom_call_target="tpu_custom_call" | custom-call | tf_op jit(solution)/shard_map/pack/pallas_call | solution.py:209
  2.3 18.4 %all-to-all-start = ((bf16[128,2,768]{2,1,0:T(2,128)(2,1)}), bf16[128,2,768]{2,1,0:T(2,128)(2,1)S(1)}, u32[]{:S(2)}, u32[]{:S(2)}) async-start(bf16[128,2,768]{2,1,0:T(2,128)(2,1)} %pack.1), calls=%async_computation | async-start | bytes 786432 | tf_op jit(solution)/shard_map/all_to_all | solution.py:216
  20.7 2.9 %prepare.1.refs_2_ = bf16[16,272,128]{2,1,0:T(8,128)(2,1)} custom-call(s32[32]{0:T(128)} %refs_0_.3, f32[32]{0:T(128)} %bitcast.3, f32[32]{0:T(128)} %bitcast.4, bf16[32,64,128]{2,1,0:T(8,128)(2,1)} %refs_3_.1, bf16[32,64,128]{2,1,0:T(8,128)(2,1)} %refs_4_.1), custom_call_target="tpu_custom_call" | custom-call | tf_op jit(solution)/shard_map/prepare/pallas_call | solution.py:225
  23.6 0.0 copy-start
  23.6 15.2 %all-to-all-done = bf16[128,2,768]{2,1,0:T(2,128)(2,1)S(1)} async-done(((bf16[128,2,768]{2,1,0:T(2,128)(2,1)}), bf16[128,2,768]{2,1,0:T(2,128)(2,1)S(1)}, u32[]{:S(2)}, u32[]{:S(2)}) %all-to-all-start) | async-done | bytes 393248 | tf_op jit(solution)/shard_map/all_to_all | solution.py:216
  38.8 3.6 %all-to-all-start.1 = ((bf16[16,272,128]{2,1,0:T(8,128)(2,1)}), bf16[16,272,128]{2,1,0:T(8,128)(2,1)S(1)}, u32[]{:S(2)}, u32[]{:S(2)}) async-start(bf16[16,272,128]{2,1,0:T(8,128)(2,1)} %prepare.1.refs_2_), calls=%async_computation.1 | async-start | bytes 2228224 | tf_op jit(solution)/shard_map/all_to_all | solution.py:229
  42.4 0.0 copy-done
  42.4 2.0 %collective-permute-start = (bf16[16,272,128]{2,1,0:T(8,128)(2,1)S(1)}, bf16[16,272,128]{2,1,0:T(8,128)(2,1)}, u32[]{:S(2)}, u32[]{:S(2)}) collective-permute-start(bf16[16,272,128]{2,1,0:T(8,128)(2,1)S(1)} %copy-done), channel_id=1, source_target_pairs={{0,32},{32,0},{64,96},{96,64},{128,160},{160,128},{192,224},{224,1... | collective-permute-start | bytes 3342344 | tf_op jit(solution)/shard_map/ppermute | solution.py:226
  44.4 0.9 %reshape.25.refs_1_ = bf16[256,768]{1,0:T(8,128)(2,1)} reshape(bf16[128,2,768]{2,1,0:T(2,128)(2,1)S(1)} %all-to-all-done) | data formatting | bytes 786432 | tf_op jit(solution)/shard_map/reshape | solution.py:228
  45.3 1.9 %collective-permute-done.refs_3_ = bf16[16,272,128]{2,1,0:T(8,128)(2,1)} collective-permute-done((bf16[16,272,128]{2,1,0:T(8,128)(2,1)S(1)}, bf16[16,272,128]{2,1,0:T(8,128)(2,1)}, u32[]{:S(2)}, u32[]{:S(2)}) %collective-permute-start) | collective-permute-done | bytes 1114144 | tf_op jit(solution)/shard_map/ppermute | solution.py:226
  47.2 9.3 %attend.1 = bf16[16,80,128]{2,1,0:T(8,128)(2,1)} custom-call(s32[1]{0:T(128)} %bitcast.refs_0_, bf16[256,768]{1,0:T(8,128)(2,1)} %reshape.25.refs_1_, bf16[16,272,128]{2,1,0:T(8,128)(2,1)} %prepare.1.refs_2_, bf16[16,272,128]{2,1,0:T(8,128)(2,1)} %collective-permute-done.refs_3_), custom_call_target="tpu_custom_call" | custom-call | tf_op jit(solution)/shard_map/attend/pallas_call | solution.py:244
  56.4 15.2 %all-to-all-done.1.refs_1_ = bf16[16,272,128]{2,1,0:T(8,128)(2,1)S(1)} async-done(((bf16[16,272,128]{2,1,0:T(8,128)(2,1)}), bf16[16,272,128]{2,1,0:T(8,128)(2,1)S(1)}, u32[]{:S(2)}, u32[]{:S(2)}) %all-to-all-start.1) | async-done | bytes 1114144 | tf_op jit(solution)/shard_map/all_to_all | solution.py:229
  71.7 3.5 %all-to-all-start.2 = ((bf16[16,80,128]{2,1,0:T(8,128)(2,1)}), bf16[16,80,128]{2,1,0:T(8,128)(2,1)S(1)}, u32[]{:S(2)}, u32[]{:S(2)}) async-start(bf16[16,80,128]{2,1,0:T(8,128)(2,1)} %attend.1), calls=%async_computation.2 | async-start | bytes 655360 | tf_op jit(solution)/shard_map/all_to_all | solution.py:246
  75.2 0.3 convert_reduce_fusion
  75.5 0.1 reshape.26.refs_0_
  75.6 1.7 %place.1 = (bf16[2048,128]{1,0:T(8,128)(2,1)}, bf16[2048,128]{1,0:T(8,128)(2,1)}) custom-call(s32[32]{0:T(128)S(1)} %reshape.26.refs_0_, bf16[16,272,128]{2,1,0:T(8,128)(2,1)S(1)} %all-to-all-done.1.refs_1_), custom_call_target="tpu_custom_call" | custom-call | tf_op jit(solution)/shard_map/place/pallas_call | solution.py:258
  77.3 10.8 %all-to-all-done.2.msg_ref = bf16[16,80,128]{2,1,0:T(8,128)(2,1)S(1)} async-done(((bf16[16,80,128]{2,1,0:T(8,128)(2,1)}), bf16[16,80,128]{2,1,0:T(8,128)(2,1)S(1)}, u32[]{:S(2)}, u32[]{:S(2)}) %all-to-all-start.2) | async-done | bytes 327712 | tf_op jit(solution)/shard_map/all_to_all | solution.py:246
  88.2 1.0 %combine.1 = bf16[16,1024]{1,0:T(8,128)(2,1)} custom-call(bf16[16,80,128]{2,1,0:T(8,128)(2,1)S(1)} %all-to-all-done.2.msg_ref), custom_call_target="tpu_custom_call" | custom-call | tf_op jit(solution)/shard_map/combine/pallas_call | solution.py:259
Async XLA Ops:
  2.3 36.5 %all-to-all-start = ((bf16[128,2,768]{2,1,0:T(2,128)(2,1)}), bf16[128,2,768]{2,1,0:T(2,128)(2,1)S(1)}, u32[]{:S(2)}, u32[]{:S(2)}) async-start(bf16[128,2,768]{2,1,0:T(2,128)(2,1)} %pack.1), calls=%async_computation | async-start | bytes 786432 | tf_op jit(solution)/shard_map/all_to_all | solution.py:216
  23.6 18.8 %copy-start = (bf16[16,272,128]{2,1,0:T(8,128)(2,1)S(1)}, bf16[16,272,128]{2,1,0:T(8,128)(2,1)}, u32[]{:S(2)}) copy-start(bf16[16,272,128]{2,1,0:T(8,128)(2,1)} %prepare.1.refs_2_) | copy-start | bytes 3342340
  38.8 32.9 %all-to-all-start.1 = ((bf16[16,272,128]{2,1,0:T(8,128)(2,1)}), bf16[16,272,128]{2,1,0:T(8,128)(2,1)S(1)}, u32[]{:S(2)}, u32[]{:S(2)}) async-start(bf16[16,272,128]{2,1,0:T(8,128)(2,1)} %prepare.1.refs_2_), calls=%async_computation.1 | async-start | bytes 2228224 | tf_op jit(solution)/shard_map/all_to_all | solution.py:229
  42.4 4.8 %collective-permute-start = (bf16[16,272,128]{2,1,0:T(8,128)(2,1)S(1)}, bf16[16,272,128]{2,1,0:T(8,128)(2,1)}, u32[]{:S(2)}, u32[]{:S(2)}) collective-permute-start(bf16[16,272,128]{2,1,0:T(8,128)(2,1)S(1)} %copy-done), channel_id=1, source_target_pairs={{0,32},{32,0},{64,96},{96,64},{128,160},{160,128},{192,224},{224,1... | collective-permute-start | bytes 3342344 | tf_op jit(solution)/shard_map/ppermute | solution.py:226
  71.7 16.5 %all-to-all-start.2 = ((bf16[16,80,128]{2,1,0:T(8,128)(2,1)}), bf16[16,80,128]{2,1,0:T(8,128)(2,1)S(1)}, u32[]{:S(2)}, u32[]{:S(2)}) async-start(bf16[16,80,128]{2,1,0:T(8,128)(2,1)} %attend.1), calls=%async_computation.2 | async-start | bytes 655360 | tf_op jit(solution)/shard_map/all_to_all | solution.py:246
